TPU v7x, 32 devices: a whole 2x2x4 slice. The times are simulated.
32 devices in a mesh: shard: 4 (over z), ctx: 2 (over core), tp: 4 (over y, x).
Axes of the slice: x: 2, y: 2, z: 4, core: 2. Of those that a mesh axis runs over, the one named last changes fastest.
Arguments:
- tokens: bfloat16 [8, 2048, 768], P('shard', 'ctx'), may hold values from -6 to 6
- segment_ids: int32 [8, 2048], P('shard', 'ctx'), may hold values from 0 to 34, as said below
- offsets: int32 [8, 2048], P('shard', 'ctx'), may hold values from 0 to 799, as said below
- qkv_weight: bfloat16 [768, 3, 768], P(('shard', 'ctx'), None, 'tp'), may hold values from -0.3125 to 0.3125
- out_weight: bfloat16 [768, 768], P(('shard', 'ctx'), 'tp'), may hold values from -0.875 to 0.875
- ffn_weight: bfloat16 [768, 2, 3072], P(('shard', 'ctx'), None, 'tp'), may hold values from -0.21875 to 0.21875
- qkv_bias: float32 [3, 768], P(None, 'tp'), may hold values from -3 to 3
- ffn_bias: float32 [3072], P('tp'), may hold values from -3 to 3
- norm_gain: float32 [2, 768], replicated, may hold values from 0.5 to 1.5
- shift_params: float32 [4, 768], replicated, may hold values from -3 to 3
- out_grad: bfloat16 [8, 2048, 768], P('shard', 'ctx'), may hold values from -6 to 6
Outputs:
- outputs: bfloat16 [8, 2048, 768], P('shard', 'ctx')
- grad_tokens: bfloat16 [8, 2048, 768], P('shard', 'ctx')
- grad_qkv_weight: float32 [768, 3, 768], P(('shard', 'ctx'), None, 'tp')
- grad_out_weight: float32 [768, 768], P(('shard', 'ctx'), 'tp')
- grad_ffn_weight: float32 [768, 2, 3072], P(('shard', 'ctx'), None, 'tp')
- grad_qkv_bias: float32 [3, 768], P(None, 'tp')
- grad_ffn_bias: float32 [3072], P('tp')
- grad_norm_gain: float32 [2, 768], replicated
- grad_shift_params: float32 [4, 768], replicated
Inputs may be any that keep to these rules, and one draw needn't show every extreme that they name: `segment_ids`: segment numbers start at 0 in each sequence and rise by one where a new document begins. offsets are 0 at a document's first token and rise by one along it; a document has at most 800 tokens, and every document but a sequence's last has at least 60.
All inputs are finite; a program needn't handle non-finite values.
Results may differ from a plain program's by a relative error of at most 0.017.
The roundings to bfloat16 on the way count: a program that leaves them out, or rounds other values in their place, can miss the bound.
Values may be sent and summed in bfloat16 or wider, within the bound.
No kernel may reach another device: no remote copies, remote signals or barrier semaphores. Data moves between devices by JAX's collectives and lax.ppermute only.
A program may use at most 192 MiB of HBM per device.

v0:
```python
from functools import partial
import jax
import jax.numpy as jnp
from jax import lax
from jax.sharding import PartitionSpec as P

HEAD = 64
EPSILON = 1e-12


def rotate_pairs(values, offsets, direction):
    half_size = values.shape[-1] // 2
    frequency = 10000.0 ** (-2.0 * jnp.arange(half_size, dtype=jnp.float32) / values.shape[-1])
    angles = offsets.astype(jnp.float32)[:, None] * frequency[None, :]
    cosine = jnp.cos(angles)[:, None, :]
    sine_part = direction * jnp.sin(angles)[:, None, :]
    paired = values.reshape(values.shape[:-1] + (half_size, 2))
    even_part = paired[..., 0]
    odd_part = paired[..., 1]
    turned = jnp.stack(
        [even_part * cosine - odd_part * sine_part, even_part * sine_part + odd_part * cosine],
        axis=-1,
    )
    return turned.reshape(values.shape)


def norm_parts(rows_in):
    centre = rows_in - jnp.mean(rows_in, axis=-1, keepdims=True)
    inverse_root = lax.rsqrt(jnp.mean(centre * centre, axis=-1, keepdims=True) + EPSILON)
    return (centre * inverse_root, inverse_root)


def norm_back(grad_in, scaled, inverse_root, gain_row):
    grad_scaled = grad_in * gain_row
    term_mean = jnp.mean(grad_scaled, axis=-1, keepdims=True)
    term_along = jnp.mean(grad_scaled * scaled, axis=-1, keepdims=True)
    return inverse_root * (grad_scaled - term_mean - scaled * term_along)


def attention_weights(qkv_weight, out_weight):
    return (
        lax.all_gather(qkv_weight, ("shard", "ctx"), axis=0, tiled=True),
        lax.all_gather(out_weight, ("shard", "ctx"), axis=0, tiled=True),
    )


def feed_weights(ffn_weight):
    return lax.all_gather(ffn_weight, ("shard", "ctx"), axis=0, tiled=True)


def masked_scores(queries, keys_all, same_doc, score_scale):
    scores = (
        jnp.einsum("shd,thd->hst", queries, keys_all, preferred_element_type=jnp.float32)
        * score_scale
    )
    return jnp.where(same_doc, scores, -1e30)


def contract_last(left, right):
    return lax.dot_general(
        left, right, (((1,), (1,)), ((), ())), preferred_element_type=jnp.float32
    )


def contract_first(left, right):
    return lax.dot_general(
        left, right, (((0,), (0,)), ((), ())), preferred_element_type=jnp.float32
    )


def body(
    tokens,
    segment_ids,
    offsets,
    qkv_weight,
    out_weight,
    ffn_weight,
    qkv_bias,
    ffn_bias,
    norm_gain,
    shift_params,
    out_grad,
):
    model_width = tokens.shape[2]
    part_width = qkv_weight.shape[2]
    hidden_width = ffn_weight.shape[2]
    local_heads = part_width // HEAD
    score_scale = HEAD ** (-0.5)
    tp_count = lax.axis_size("tp")
    tp_rank = lax.axis_index("tp")

    def micro_step(totals, micro_batch):
        tokens_mb, segment_mb, offsets_mb, grad_mb = micro_batch
        half_len = tokens_mb.shape[0]
        share_len = half_len // tp_count
        share_start = tp_rank * share_len

        def share_rows(rows):
            return lax.dynamic_slice_in_dim(rows, share_start, share_len, 0)

        qkv_full, out_full = attention_weights(qkv_weight, out_weight)
        ffn_full = feed_weights(ffn_weight)
        projected = (
            jnp.einsum("sd,dke->kse", tokens_mb, qkv_full, preferred_element_type=jnp.float32)
            + qkv_bias[:, None, :]
        )
        per_head = projected.reshape(3, half_len, local_heads, HEAD)
        queries = rotate_pairs(per_head[0], offsets_mb, 1.0).astype(jnp.bfloat16)
        keys_own = rotate_pairs(per_head[1], offsets_mb, 1.0).astype(jnp.bfloat16)
        values_own = per_head[2].astype(jnp.bfloat16)
        pair_own = jnp.stack([keys_own, values_own]).reshape(2, half_len, part_width)
        segment_own = segment_mb.astype(jnp.bfloat16)
        pair_all, segment_all = (
            lax.all_gather(pair_own, "ctx", axis=1, tiled=True),
            lax.all_gather(segment_own, "ctx", axis=0, tiled=True),
        )
        seq_len = pair_all.shape[1]
        keys_all = pair_all[0].reshape(seq_len, local_heads, HEAD)
        values_all = pair_all[1].reshape(seq_len, local_heads, HEAD)
        same_doc = (segment_own[:, None] == segment_all[None, :])[None]
        scores = masked_scores(queries, keys_all, same_doc, score_scale)
        row_top = jnp.max(scores, axis=-1, keepdims=True)
        exponent = jnp.exp(scores - row_top)
        row_total = jnp.sum(exponent, axis=-1, keepdims=True)
        probs_b = (exponent / row_total).astype(jnp.bfloat16)
        log_total = row_top + jnp.log(row_total)
        context = jnp.einsum(
            "hst,thd->shd", probs_b, values_all, preferred_element_type=jnp.float32
        )
        context = context.reshape(half_len, part_width).astype(jnp.bfloat16)
        attended = lax.psum(contract_last(context, out_full), "tp")
        first_scaled, first_root = norm_parts(
            tokens_mb.astype(jnp.float32) + attended + shift_params[2]
        )
        normed = first_scaled * norm_gain[0] + shift_params[0]
        normed_b = normed.astype(jnp.bfloat16)
        hidden_in = (
            jnp.dot(normed_b, ffn_full[:, 0, :], preferred_element_type=jnp.float32) + ffn_bias
        )
        activated, gelu_pull = jax.vjp(partial(jax.nn.gelu, approximate=False), hidden_in)
        activated_b = activated.astype(jnp.bfloat16)
        returned = lax.psum(contract_last(activated_b, ffn_full[:, 1, :]), "tp")
        second_scaled, second_root = norm_parts(normed + returned + shift_params[3])
        layer_out = (second_scaled * norm_gain[1] + shift_params[1]).astype(jnp.bfloat16)
        qkv_back, out_back = attention_weights(qkv_weight, out_weight)
        ffn_back = feed_weights(ffn_weight)
        grad_top = grad_mb.astype(jnp.float32)
        grad_gain_two = jnp.sum(share_rows(grad_top) * share_rows(second_scaled), axis=0)
        grad_second = norm_back(grad_top, second_scaled, second_root, norm_gain[1])
        grad_second_b = grad_second.astype(jnp.bfloat16)
        grad_down = contract_first(grad_second_b, activated_b)
        grad_act = jnp.dot(grad_second_b, ffn_back[:, 1, :], preferred_element_type=jnp.float32)
        grad_hidden = gelu_pull(grad_act)[0].astype(jnp.bfloat16)
        grad_up = contract_first(normed_b, grad_hidden)
        grad_ffn_bias = jnp.sum(grad_hidden.astype(jnp.float32), axis=0)
        ffn_part = contract_last(grad_hidden, ffn_back[:, 0, :])
        grad_normed = grad_second + lax.psum(ffn_part, "tp")
        grad_first = norm_back(grad_normed, first_scaled, first_root, norm_gain[0])
        grad_first_b = grad_first.astype(jnp.bfloat16)
        normed_part = share_rows(grad_normed)
        first_part = share_rows(grad_first)
        grad_gain_one = jnp.sum(normed_part * share_rows(first_scaled), axis=0)
        grad_out_proj = contract_first(grad_first_b, context)
        grad_context = jnp.dot(grad_first_b, out_back, preferred_element_type=jnp.float32).astype(
            jnp.bfloat16
        )
        grad_context = grad_context.reshape(half_len, local_heads, HEAD)
        scores_again = masked_scores(queries, keys_all, same_doc, score_scale)
        probs = jnp.exp(scores_again - log_total)
        probs_again = probs.astype(jnp.bfloat16)
        grad_probs = jnp.einsum(
            "shd,thd->hst", grad_context, values_all, preferred_element_type=jnp.float32
        )
        row_dot = jnp.sum(probs * grad_probs, axis=-1, keepdims=True)
        grad_scores = (probs * (grad_probs - row_dot)).astype(jnp.bfloat16)
        grad_queries = (
            jnp.einsum("hst,thd->shd", grad_scores, keys_all, preferred_element_type=jnp.float32)
            * score_scale
        )
        grad_keys = (
            jnp.einsum("hst,shd->thd", grad_scores, queries, preferred_element_type=jnp.float32)
            * score_scale
        )
        grad_values = jnp.einsum(
            "hst,shd->thd", probs_again, grad_context, preferred_element_type=jnp.float32
        )
        grad_pair = lax.psum_scatter(
            jnp.stack([grad_keys, grad_values]).reshape(2, seq_len, part_width),
            "ctx",
            scatter_dimension=1,
            tiled=True,
        )
        grad_pair = grad_pair.reshape(2, half_len, local_heads, HEAD)
        grad_proj = jnp.stack(
            [
                rotate_pairs(grad_queries, offsets_mb, -1.0),
                rotate_pairs(grad_pair[0], offsets_mb, -1.0),
                grad_pair[1],
            ]
        )
        grad_proj = grad_proj.reshape(3, half_len, part_width).astype(jnp.bfloat16)
        grad_qkv_bias = jnp.sum(grad_proj.astype(jnp.float32), axis=1)
        grad_qkv = jnp.einsum(
            "sd,kse->dke", tokens_mb, grad_proj, preferred_element_type=jnp.float32
        )
        grad_branch = jnp.einsum(
            "kse,dke->sd", grad_proj, qkv_back, preferred_element_type=jnp.float32
        )
        grad_inputs = (grad_first + lax.psum(grad_branch, "tp")).astype(jnp.bfloat16)
        grad_shift = jnp.stack(
            [
                jnp.sum(normed_part, axis=0),
                jnp.sum(share_rows(grad_top), axis=0),
                jnp.sum(first_part, axis=0),
                jnp.sum(share_rows(grad_second), axis=0),
            ]
        )
        grad_gain = jnp.stack([grad_gain_one, grad_gain_two])
        grad_ffn = jnp.stack([grad_up, grad_down], axis=1)
        updated = (
            totals[0] + grad_qkv,
            totals[1] + grad_out_proj,
            totals[2] + grad_ffn,
            totals[3] + grad_qkv_bias,
            totals[4] + grad_ffn_bias,
            totals[5] + grad_gain,
            totals[6] + grad_shift,
        )
        return (updated, (layer_out, grad_inputs))

    zero_grads = (
        jnp.zeros((model_width, 3, part_width), jnp.float32),
        jnp.zeros((model_width, part_width), jnp.float32),
        jnp.zeros((model_width, 2, hidden_width), jnp.float32),
        jnp.zeros((3, part_width), jnp.float32),
        jnp.zeros((hidden_width,), jnp.float32),
        jnp.zeros((2, model_width), jnp.float32),
        jnp.zeros((4, model_width), jnp.float32),
    )
    totals, (outputs, grad_tokens) = lax.scan(
        micro_step, zero_grads, (tokens, segment_ids, offsets, out_grad)
    )
    grad_qkv_weight, grad_out_weight, grad_ffn_weight = (
        lax.psum_scatter(totals[0], ("shard", "ctx"), scatter_dimension=0, tiled=True),
        lax.psum_scatter(totals[1], ("shard", "ctx"), scatter_dimension=0, tiled=True),
        lax.psum_scatter(totals[2], ("shard", "ctx"), scatter_dimension=0, tiled=True),
    )
    placed_qkv = lax.dynamic_update_slice(
        jnp.zeros((3, part_width * tp_count), jnp.float32),
        totals[3],
        (jnp.int32(0), tp_rank * part_width),
    )
    placed_ffn = lax.dynamic_update_slice(
        jnp.zeros((hidden_width * tp_count,), jnp.float32), totals[4], (tp_rank * hidden_width,)
    )
    summed_qkv, summed_ffn, grad_norm_gain, grad_shift_params = lax.psum(
        (placed_qkv, placed_ffn, totals[5], totals[6]), ("shard", "ctx", "tp")
    )
    grad_qkv_bias = lax.dynamic_slice_in_dim(summed_qkv, tp_rank * part_width, part_width, 1)
    grad_ffn_bias = lax.dynamic_slice_in_dim(summed_ffn, tp_rank * hidden_width, hidden_width, 0)
    return (
        outputs,
        grad_tokens,
        grad_qkv_weight,
        grad_out_weight,
        grad_ffn_weight,
        grad_qkv_bias,
        grad_ffn_bias,
        grad_norm_gain,
        grad_shift_params,
    )


def solution(mesh):
    return jax.shard_map(
        body,
        mesh=mesh,
        in_specs=(
            P("shard", "ctx", None),
            P("shard", "ctx"),
            P("shard", "ctx"),
            P(("shard", "ctx"), None, "tp"),
            P(("shard", "ctx"), "tp"),
            P(("shard", "ctx"), None, "tp"),
            P(None, "tp"),
            P("tp"),
            P(),
            P(),
            P("shard", "ctx", None),
        ),
        out_specs=(
            P("shard", "ctx", None),
            P("shard", "ctx", None),
            P(("shard", "ctx"), None, "tp"),
            P(("shard", "ctx"), "tp"),
            P(("shard", "ctx"), None, "tp"),
            P(None, "tp"),
            P("tp"),
            P(),
            P(),
        ),
        check_vma=False,
    )
```

profile of v0, /device:TPU:0, one launch (start us, length us, event | category | flops | bytes accessed | tf_op | source)
XLA Modules:
  0.0 1406.7 jit_solution(18068525269604240569)
XLA Ops:
  10.9 1200.5 %while.29 = (s32[]{:T(128)}, f32[768,3,192]{0,2,1:T(8,128)}, f32[768,192]{0,1:T(8,128)}, f32[768,2,768]{2,0,1:T(8,128)}, f32[3,192]{1,0:T(4,128)}, /*index=5*/f3...) while((s32[]{:T(128)}, f32[768,3,192]{0,2,1:T(8,128)}, ...), condition=%wide.region_25.26_spmd.clone, body=%wide.region_0.25_spmd.clone.sunk | while | flops 15947476992 | bytes 964769600 | solution.py:240
  10.9 23.1 %all_gather.42 = bf16[768,3,192]{2,1,0:T(4,128)(2,1)} all-gather(bf16[96,3,192]{2,1,0:T(4,128)(2,1)S(1)} %get-tuple-element.828), channel_id=1, replica_groups=mesh['shard'=4,'ctx'=2,'tp'=4] {'shard','ctx'}, dimensions={0}, use_global_device_ids=true | all-gather | bytes 995328 | tf_op jit(solution)/shard_map/while/body/eval_jaxpr/all_gather | solution.py:42
  63.8 16.3 %all_gather.41 = bf16[768,192]{1,0:T(8,128)(2,1)} all-gather(bf16[96,192]{1,0:T(8,128)(2,1)} %get-tuple-element.832), channel_id=1, replica_groups=mesh['shard'=4,'ctx'=2,'tp'=4] {'shard','ctx'}, dimensions={0}, use_global_device_ids=true | all-gather | bytes 331776 | tf_op jit(solution)/shard_map/while/body/eval_jaxpr/all_gather | solution.py:43
  122.3 84.8 %all-reduce.10.cloned.1.call-done = f32[1024,768]{1,0:T(8,128)} async-done(((f32[1024,768]{1,0:T(8,128)}), f32[1024,768]{1,0:T(8,128)}) %all-reduce.10.cloned.1.call-update) | async-done | bytes 3145744 | tf_op jit(solution)/shard_map/while/body/eval_jaxpr/psum | solution.py:131
  228.0 87.1 %all-reduce.12.cloned.1.call-done = f32[1024,768]{1,0:T(8,128)} async-done(((f32[1024,768]{1,0:T(8,128)}), f32[1024,768]{1,0:T(8,128)}) %all-reduce.12.cloned.1.call-update) | async-done | bytes 3145744 | tf_op jit(solution)/shard_map/while/body/eval_jaxpr/psum | solution.py:142
  335.9 86.1 %all-reduce.14.cloned.1.call-done = f32[1024,768]{1,0:T(8,128)} async-done(((f32[1024,768]{1,0:T(8,128)}), f32[1024,768]{1,0:T(8,128)}) %all-reduce.14.cloned.1.call-update) | async-done | bytes 3145744 | tf_op jit(solution)/shard_map/while/body/eval_jaxpr/psum | solution.py:157
  430.4 11.4 fusion.160
  441.8 16.4 %multiply_reduce_fusion.14 = (f32[3,1024]{1,0:T(4,128)}, f32[3,1024,2048]{2,1,0:T(8,128)}) fusion(f32[3,1024,2048]{2,1,0:T(8,128)} %get-tuple-element.731, f32[3,1024]{1,0:T(4,128)S(1)} %log_add_fusion.2, bf16[1024,3,64]{0,2,1:T(8,128)(2,1)} %bitcast.223, bf16[2048,3,64]{0,2,1:T(8,128)(2,1)} %bitcast.227), kind=kOutput, calls=%fused_computation.1.clone.1 | convolution fusion | flops 824177664 | bytes 51535872 | tf_op jit(solution)/shard_map/while/body/eval_jaxpr/shd,thd->hst/dot_general | solution.py:171
  458.2 16.8 %multiply_convert_fusion.5 = bf16[3,1024,2048]{2,1,0:T(8,128)(2,1)S(1)} fusion(f32[3,1024,2048]{2,1,0:T(8,128)} %get-tuple-element.750, f32[3,1024,2048]{2,1,0:T(8,128)} %get-tuple-element.731, f32[3,1024]{1,0:T(4,128)} %get-tuple-element.751, f32[3,1024]{1,0:T(4,128)S(1)} %log_add_fusion.2), kind=kLoop, calls=%fused_computation.clone.1 | loop fusion | flops 25165824 | bytes 62939136 | tf_op jit(solution)/shard_map/while/body/eval_jaxpr/convert_element_type | solution.py:175
  536.2 70.3 %all-reduce.16.cloned.1.call-done = f32[1024,768]{1,0:T(8,128)} async-done(((f32[1024,768]{1,0:T(8,128)}), f32[1024,768]{1,0:T(8,128)}) %all-reduce.16.cloned.1.call-update) | async-done | bytes 3145744 | tf_op jit(solution)/shard_map/while/body/eval_jaxpr/psum | solution.py:209
  610.1 21.4 %all_gather.42 = bf16[768,3,192]{2,1,0:T(4,128)(2,1)} all-gather(bf16[96,3,192]{2,1,0:T(4,128)(2,1)S(1)} %get-tuple-element.828), channel_id=1, replica_groups=mesh['shard'=4,'ctx'=2,'tp'=4] {'shard','ctx'}, dimensions={0}, use_global_device_ids=true | all-gather | bytes 995328 | tf_op jit(solution)/shard_map/while/body/eval_jaxpr/all_gather | solution.py:42
  661.3 16.0 %all_gather.41 = bf16[768,192]{1,0:T(8,128)(2,1)} all-gather(bf16[96,192]{1,0:T(8,128)(2,1)} %get-tuple-element.832), channel_id=1, replica_groups=mesh['shard'=4,'ctx'=2,'tp'=4] {'shard','ctx'}, dimensions={0}, use_global_device_ids=true | all-gather | bytes 331776 | tf_op jit(solution)/shard_map/while/body/eval_jaxpr/all_gather | solution.py:43
  719.7 83.5 %all-reduce.10.cloned.1.call-done = f32[1024,768]{1,0:T(8,128)} async-done(((f32[1024,768]{1,0:T(8,128)}), f32[1024,768]{1,0:T(8,128)}) %all-reduce.10.cloned.1.call-update) | async-done | bytes 3145744 | tf_op jit(solution)/shard_map/while/body/eval_jaxpr/psum | solution.py:131
  808.3 11.2 multiply_convert_fusion.4
  824.1 87.2 %all-reduce.12.cloned.1.call-done = f32[1024,768]{1,0:T(8,128)} async-done(((f32[1024,768]{1,0:T(8,128)}), f32[1024,768]{1,0:T(8,128)}) %all-reduce.12.cloned.1.call-update) | async-done | bytes 3145744 | tf_op jit(solution)/shard_map/while/body/eval_jaxpr/psum | solution.py:142
  931.9 86.4 %all-reduce.14.cloned.1.call-done = f32[1024,768]{1,0:T(8,128)} async-done(((f32[1024,768]{1,0:T(8,128)}), f32[1024,768]{1,0:T(8,128)}) %all-reduce.14.cloned.1.call-update) | async-done | bytes 3145744 | tf_op jit(solution)/shard_map/while/body/eval_jaxpr/psum | solution.py:157
  1026.6 11.4 fusion.160
  1038.0 16.4 %multiply_reduce_fusion.14 = (f32[3,1024]{1,0:T(4,128)}, f32[3,1024,2048]{2,1,0:T(8,128)}) fusion(f32[3,1024,2048]{2,1,0:T(8,128)} %get-tuple-element.731, f32[3,1024]{1,0:T(4,128)S(1)} %log_add_fusion.2, bf16[1024,3,64]{0,2,1:T(8,128)(2,1)} %bitcast.223, bf16[2048,3,64]{0,2,1:T(8,128)(2,1)} %bitcast.227), kind=kOutput, calls=%fused_computation.1.clone.1 | convolution fusion | flops 824177664 | bytes 51535872 | tf_op jit(solution)/shard_map/while/body/eval_jaxpr/shd,thd->hst/dot_general | solution.py:171
  1054.4 16.8 %multiply_convert_fusion.5 = bf16[3,1024,2048]{2,1,0:T(8,128)(2,1)S(1)} fusion(f32[3,1024,2048]{2,1,0:T(8,128)} %get-tuple-element.750, f32[3,1024,2048]{2,1,0:T(8,128)} %get-tuple-element.731, f32[3,1024]{1,0:T(4,128)} %get-tuple-element.751, f32[3,1024]{1,0:T(4,128)S(1)} %log_add_fusion.2), kind=kLoop, calls=%fused_computation.clone.1 | loop fusion | flops 25165824 | bytes 62939136 | tf_op jit(solution)/shard_map/while/body/eval_jaxpr/convert_element_type | solution.py:175
  1134.2 68.6 %all-reduce.16.cloned.1.call-done = f32[1024,768]{1,0:T(8,128)} async-done(((f32[1024,768]{1,0:T(8,128)}), f32[1024,768]{1,0:T(8,128)}) %all-reduce.16.cloned.1.call-update) | async-done | bytes 3145744 | tf_op jit(solution)/shard_map/while/body/eval_jaxpr/psum | solution.py:209
  1225.5 42.1 %all-reduce.1 = (f32[3,768]{1,0:T(4,128)S(1)}, f32[3072]{0:T(1024)S(1)}, f32[2,768]{1,0:T(2,128)}, f32[4,768]{1,0:T(4,128)}) all-reduce(f32[3,768]{1,0:T(4,128)S(1)} %dynamic_update_slice.19, f32[3072]{0:T(1024)S(1)} %dynamic_update_slice.20, ...), channel_id=1, replica_groups=mesh['shard'=4,'ctx'=2,'tp'=4] {'shard','ctx','tp'}, use_global_device_ids=true, to_apply=%region_29.30 | all-reduce | flops 9984 | bytes 79872 | tf_op jit(solution)/shard_map/psum | solution.py:256
  1270.2 56.7 %all-reduce.8.cloned.1.call-done = f32[768,2,768]{2,1,0:T(2,128)} async-done(((f32[768,2,768]{2,1,0:T(2,128)}), f32[768,2,768]{2,1,0:T(2,128)}) %all-reduce.8.cloned.1.call-update) | async-done | bytes 4718608
  1328.8 32.5 %reduce-scatter.6.cloned.1.call-done = f32[96,192]{1,0:T(8,128)} async-done(((f32[768,192]{1,0:T(8,128)}), f32[96,192]{1,0:T(8,128)}) %reduce-scatter.6.cloned.1.call-update) | async-done | bytes 73744 | tf_op jit(solution)/shard_map/reduce_scatter | solution.py:245
  1361.3 37.6 %reduce-scatter.4.cloned.1.call-done = f32[96,3,192]{2,0,1:T(8,128)} async-done(((f32[768,3,192]{2,0,1:T(8,128)}), f32[96,3,192]{2,0,1:T(8,128)}) %reduce-scatter.4.cloned.1.call-update) | async-done | bytes 221200 | tf_op jit(solution)/shard_map/reduce_scatter | solution.py:244
  (527 shorter events, 382.8 us)
Async XLA Ops:
  10.9 71.7 %all-gather.7.cloned.1.call-start = ((), (), s32[]{:S(2)}) async-start(), calls=%async_computation.6 | async-start | bytes 2359296 | tf_op jit(solution)/shard_map/while/body/eval_jaxpr/all_gather | solution.py:114
  57.9 149.1 %all-reduce.10.cloned.1.call-start = ((), (), s32[]{:S(2)}) async-start(), calls=%async_computation.7 | async-start | bytes 6291456 | tf_op jit(solution)/shard_map/while/body/eval_jaxpr/psum | solution.py:131
  119.9 92.2 %all-gather.9.cloned.1.call-start = ((), (), s32[]{:S(2)}) async-start(), calls=%async_computation.8 | async-start | bytes 2654208 | tf_op jit(solution)/shard_map/while/body/eval_jaxpr/all_gather | solution.py:48
  120.5 194.6 %all-reduce.12.cloned.1.call-start = ((), (), s32[]{:S(2)}) async-start(), calls=%async_computation.9 | async-start | bytes 6291456 | tf_op jit(solution)/shard_map/while/body/eval_jaxpr/psum | solution.py:142
  120.8 194.3 %copy-start.35 = (f32[768]{0:T(1024)}, f32[768]{0:T(1024)S(1)}, u32[]{:S(2)}) copy-start(f32[768]{0:T(1024)S(1)} %get-tuple-element.733) | copy-start | bytes 9220 | tf_op jit(solution)/shard_map/while
  122.3 192.8 %copy-start.45 = (f32[768]{0:T(1024)}, f32[768]{0:T(1024)S(1)}, u32[]{:S(2)}) copy-start(f32[768]{0:T(1024)S(1)} %get-tuple-element.737) | copy-start | bytes 9220 | tf_op jit(solution)/shard_map/while
  227.7 87.4 %copy-start.48 = (f32[768]{0:T(1024)S(1)}, f32[768]{0:T(1024)}, u32[]{:S(2)}) copy-start(f32[768]{0:T(1024)} %get-tuple-element.736) | copy-start | bytes 9220 | tf_op jit(solution)/shard_map/while
  227.7 194.3 %all-reduce.14.cloned.1.call-start = ((), (), s32[]{:S(2)}) async-start(), calls=%async_computation.10 | async-start | bytes 6291456 | tf_op jit(solution)/shard_map/while/body/eval_jaxpr/psum | solution.py:157
  334.7 163.7 %reduce-scatter.8.cloned.1.call-start = ((), (), s32[]{:S(2)}) async-start(), calls=%async_computation.11 | async-start | bytes 4718592 | tf_op jit(solution)/shard_map/while/body/eval_jaxpr/reduce_scatter | solution.py:187
  481.7 124.7 %all-reduce.16.cloned.1.call-start = ((), (), s32[]{:S(2)}) async-start(), calls=%async_computation.12 | async-start | bytes 6291456 | tf_op jit(solution)/shard_map/while/body/eval_jaxpr/psum | solution.py:209
  610.0 69.7 %all-gather.7.cloned.1.call-start = ((), (), s32[]{:S(2)}) async-start(), calls=%async_computation.6 | async-start | bytes 2359296 | tf_op jit(solution)/shard_map/while/body/eval_jaxpr/all_gather | solution.py:114
  655.4 147.8 %all-reduce.10.cloned.1.call-start = ((), (), s32[]{:S(2)}) async-start(), calls=%async_computation.7 | async-start | bytes 6291456 | tf_op jit(solution)/shard_map/while/body/eval_jaxpr/psum | solution.py:131
  717.1 91.2 %all-gather.9.cloned.1.call-start = ((), (), s32[]{:S(2)}) async-start(), calls=%async_computation.8 | async-start | bytes 2654208 | tf_op jit(solution)/shard_map/while/body/eval_jaxpr/all_gather | solution.py:48
  717.7 193.6 %all-reduce.12.cloned.1.call-start = ((), (), s32[]{:S(2)}) async-start(), calls=%async_computation.9 | async-start | bytes 6291456 | tf_op jit(solution)/shard_map/while/body/eval_jaxpr/psum | solution.py:142
  718.2 193.0 %copy-start.35 = (f32[768]{0:T(1024)}, f32[768]{0:T(1024)S(1)}, u32[]{:S(2)}) copy-start(f32[768]{0:T(1024)S(1)} %get-tuple-element.733) | copy-start | bytes 9220 | tf_op jit(solution)/shard_map/while
  719.7 191.5 %copy-start.45 = (f32[768]{0:T(1024)}, f32[768]{0:T(1024)S(1)}, u32[]{:S(2)}) copy-start(f32[768]{0:T(1024)S(1)} %get-tuple-element.737) | copy-start | bytes 9220 | tf_op jit(solution)/shard_map/while
  823.9 87.4 %copy-start.48 = (f32[768]{0:T(1024)S(1)}, f32[768]{0:T(1024)}, u32[]{:S(2)}) copy-start(f32[768]{0:T(1024)} %get-tuple-element.736) | copy-start | bytes 9220 | tf_op jit(solution)/shard_map/while
  823.9 194.3 %all-reduce.14.cloned.1.call-start = ((), (), s32[]{:S(2)}) async-start(), calls=%async_computation.10 | async-start | bytes 6291456 | tf_op jit(solution)/shard_map/while/body/eval_jaxpr/psum | solution.py:157
  930.8 163.7 %reduce-scatter.8.cloned.1.call-start = ((), (), s32[]{:S(2)}) async-start(), calls=%async_computation.11 | async-start | bytes 4718592 | tf_op jit(solution)/shard_map/while/body/eval_jaxpr/reduce_scatter | solution.py:187
  1077.9 125.0 %all-reduce.16.cloned.1.call-start = ((), (), s32[]{:S(2)}) async-start(), calls=%async_computation.12 | async-start | bytes 6291456 | tf_op jit(solution)/shard_map/while/body/eval_jaxpr/psum | solution.py:209
  1131.0 71.9 %copy-start.3 = (f32[1024,768]{1,0:T(8,128)S(1)}, f32[1024,768]{1,0:T(8,128)}, u32[]{:S(2)}) copy-start(f32[1024,768]{1,0:T(8,128)} %copy-done.1) | copy-start | bytes 9437188 | tf_op jit(solution)/shard_map/while
  1211.3 115.6 %all-reduce.8.cloned.1.call-start = ((), (), s32[]{:S(2)}) async-start(), calls=%async_computation.5 | async-start | bytes 9437184
  1219.5 141.8 %reduce-scatter.6.cloned.1.call-start = ((), (), s32[]{:S(2)}) async-start(), calls=%async_computation.4 | async-start | bytes 884736 | tf_op jit(solution)/shard_map/reduce_scatter | solution.py:245
  1221.8 177.1 %reduce-scatter.4.cloned.1.call-start = ((), (), s32[]{:S(2)}) async-start(), calls=%async_computation.3 | async-start | bytes 2654208 | tf_op jit(solution)/shard_map/reduce_scatter | solution.py:244
  (139 other events, 747.8 us)
Sparse Core Ops, SparseCore 0:
  58.0 9.4 all-gather.6
  120.0 86.9 all-reduce.9
  227.8 87.2 all-reduce.11
  334.8 87.1 all-reduce.13
  481.9 10.8 reduce-scatter.7
  519.3 87.1 all-reduce.15
  655.5 8.5 all-gather.6
  717.2 85.9 all-reduce.9
  824.0 87.2 all-reduce.11
  931.0 87.2 all-reduce.13
  1078.1 10.8 reduce-scatter.7
  1115.7 87.1 all-reduce.15
Sparse Core Ops, SparseCore 1:
  122.6 31.1 all-gather.8
  719.7 30.1 all-gather.8
  1219.6 107.2 all-reduce.7
  1329.8 31.5 reduce-scatter.5
  1364.3 34.5 reduce-scatter.3
where the time goes:
time: 1410 us
  waiting for transfers between devices  782 us (55%)
  matrix products  197 us (14%)
  other arithmetic  160 us (11%)
  blocking collectives  123 us (9%)
  local copies, waits for them, and re-layouts  119 us (8%)
  between operations  16.7 us (1%)
    psum x2, waiting for transfers between devices, micro_step(): returned = lax.psum(contract_last(activated_b, ffn_full[:, 1, :]), 'tp')  174 us
    psum x2, waiting for transfers between devices, micro_step(): grad_normed = grad_second + lax.psum(ffn_part, 'tp')  172 us
    psum x2, waiting for transfers between devices, micro_step(): attended = lax.psum(contract_last(context, out_full), 'tp')  168 us
    psum x2, waiting for transfers between devices, micro_step(): lax.psum(grad_branch, 'tp')  139 us
    unnamed x4, waiting for transfers between devices  56.7 us
    all_gather x2, blocking collectives, attention_weights(): lax.all_gather(qkv_weight, ('shard', 'ctx'), axis=0, tiled=True)  44.4 us
    while x280, local copies, waits for them, and re-layouts  43.6 us
    psum x1, blocking collectives, body(): lax.psum((placed_qkv, placed_ffn, totals[5], totals[6]), ('shard', 'ctx',...  42.1 us
  transfers between devices with their start and end apart: 17, of which 11 were waited for; matrix products, arithmetic and copies ran while one was open for 7% of the time, Pallas kernels for 0%

commit v1 on v0

--- a/solution.py
+++ b/solution.py
@@ -206,7 +206,9 @@
         grad_branch = jnp.einsum(
             "kse,dke->sd", grad_proj, qkv_back, preferred_element_type=jnp.float32
         )
-        grad_inputs = (grad_first + lax.psum(grad_branch, "tp")).astype(jnp.bfloat16)
+        grad_inputs = (grad_first + jnp.sum(lax.all_gather(grad_branch, "tp"), axis=0)).astype(
+            jnp.bfloat16
+        )
         grad_shift = jnp.stack(
             [
                 jnp.sum(normed_part, axis=0),

time: 1410 us -> 1490 us (1.057)
  waiting for transfers between devices: 782 us -> 854 us
    all_gather x0 -> x2, waiting for transfers between devices: none -> 211 us  [micro_step(): lax.all_gather(grad_branch, 'tp')]
    psum x2 -> x0, waiting for transfers between devices: 139 us -> none  [micro_step(): lax.psum(grad_branch, 'tp')]
    reduce_sum x0 -> x2, other arithmetic: none -> 15.2 us  [micro_step(): jnp.sum(lax.all_gather(grad_branch, 'tp'), axis=0)]
  transfers between devices with their start and end apart: 17 -> 17, of which waited for: 11 -> 11; matrix products, arithmetic and copies ran while one was open for 7% -> 6% of each run, Pallas kernels for 0% -> 0%
where the time goes in v1:
time: 1490 us; the launch traced here: 1480 us
  waiting for transfers between devices  854 us (57%)
  matrix products  190 us (13%)
  other arithmetic  174 us (12%)
  blocking collectives  122 us (8%)
  local copies, waits for them, and re-layouts  117 us (8%)
  between operations  16.7 us (1%)
    all_gather x2, waiting for transfers between devices, micro_step(): lax.all_gather(grad_branch, 'tp')  211 us
    psum x2, waiting for transfers between devices, micro_step(): returned = lax.psum(contract_last(activated_b, ffn_full[:, 1, :]), 'tp')  174 us
    psum x2, waiting for transfers between devices, micro_step(): grad_normed = grad_second + lax.psum(ffn_part, 'tp')  173 us
    psum x2, waiting for transfers between devices, micro_step(): attended = lax.psum(contract_last(context, out_full), 'tp')  168 us
    unnamed x4, waiting for transfers between devices  56.7 us
    all_gather x2, blocking collectives, attention_weights(): lax.all_gather(qkv_weight, ('shard', 'ctx'), axis=0, tiled=True)  44.4 us
    psum x1, blocking collectives, body(): lax.psum((placed_qkv, placed_ffn, totals[5], totals[6]), ('shard', 'ctx',...  42.1 us
    while x280, local copies, waits for them, and re-layouts  41.7 us
  transfers between devices with their start and end apart: 17, of which 11 were waited for; matrix products, arithmetic and copies ran while one was open for 6% of the time, Pallas kernels for 0%

profile of v1, /device:TPU:0, one launch (start us, length us, event | category | flops | bytes accessed | tf_op | source)
XLA Modules:
  0.0 1484.4 jit_solution(11991651762972356146)
XLA Ops:
  10.9 1278.2 %while.29 = (s32[]{:T(128)}, f32[768,3,192]{0,2,1:T(8,128)}, f32[768,192]{0,1:T(8,128)}, f32[768,2,768]{2,0,1:T(8,128)}, f32[3,192]{1,0:T(4,128)}, /*index=5*/f3...) while((s32[]{:T(128)}, f32[768,3,192]{0,2,1:T(8,128)}, ...), condition=%wide.region_25.26_spmd.clone, body=%wide.region_0.25_spmd.clone.sunk | while | flops 15949049856 | bytes 1011955520 | solution.py:242
  10.9 23.1 %all_gather.54 = bf16[768,3,192]{2,1,0:T(4,128)(2,1)} all-gather(bf16[96,3,192]{2,1,0:T(4,128)(2,1)S(1)} %get-tuple-element.830), channel_id=1, replica_groups=mesh['shard'=4,'ctx'=2,'tp'=4] {'shard','ctx'}, dimensions={0}, use_global_device_ids=true | all-gather | bytes 995328 | tf_op jit(solution)/shard_map/while/body/eval_jaxpr/all_gather | solution.py:42
  63.8 16.3 %all_gather.53 = bf16[768,192]{1,0:T(8,128)(2,1)} all-gather(bf16[96,192]{1,0:T(8,128)(2,1)} %get-tuple-element.834), channel_id=1, replica_groups=mesh['shard'=4,'ctx'=2,'tp'=4] {'shard','ctx'}, dimensions={0}, use_global_device_ids=true | all-gather | bytes 331776 | tf_op jit(solution)/shard_map/while/body/eval_jaxpr/all_gather | solution.py:43
  122.3 84.8 %all-reduce.9.cloned.1.call-done = f32[1024,768]{1,0:T(8,128)} async-done(((f32[1024,768]{1,0:T(8,128)}), f32[1024,768]{1,0:T(8,128)}) %all-reduce.9.cloned.1.call-update) | async-done | bytes 3145744 | tf_op jit(solution)/shard_map/while/body/eval_jaxpr/psum | solution.py:131
  227.9 87.1 %all-reduce.11.cloned.1.call-done = f32[1024,768]{1,0:T(8,128)} async-done(((f32[1024,768]{1,0:T(8,128)}), f32[1024,768]{1,0:T(8,128)}) %all-reduce.11.cloned.1.call-update) | async-done | bytes 3145744 | tf_op jit(solution)/shard_map/while/body/eval_jaxpr/psum | solution.py:142
  335.6 86.3 %all-reduce.13.cloned.1.call-done = f32[1024,768]{1,0:T(8,128)} async-done(((f32[1024,768]{1,0:T(8,128)}), f32[1024,768]{1,0:T(8,128)}) %all-reduce.13.cloned.1.call-update) | async-done | bytes 3145744 | tf_op jit(solution)/shard_map/while/body/eval_jaxpr/psum | solution.py:157
  430.2 11.4 fusion.160
  441.6 16.4 %multiply_reduce_fusion.14 = (f32[3,1024]{1,0:T(4,128)}, f32[3,1024,2048]{2,1,0:T(8,128)}) fusion(f32[3,1024,2048]{2,1,0:T(8,128)} %get-tuple-element.731, f32[3,1024]{1,0:T(4,128)S(1)} %log_add_fusion.2, bf16[1024,3,64]{0,2,1:T(8,128)(2,1)} %bitcast.227, bf16[2048,3,64]{0,2,1:T(8,128)(2,1)} %bitcast.231), kind=kOutput, calls=%fused_computation.1.clone.1 | convolution fusion | flops 824177664 | bytes 51535872 | tf_op jit(solution)/shard_map/while/body/eval_jaxpr/shd,thd->hst/dot_general | solution.py:171
  458.0 16.8 %multiply_convert_fusion.5 = bf16[3,1024,2048]{2,1,0:T(8,128)(2,1)S(1)} fusion(f32[3,1024,2048]{2,1,0:T(8,128)} %get-tuple-element.750, f32[3,1024,2048]{2,1,0:T(8,128)} %get-tuple-element.731, f32[3,1024]{1,0:T(4,128)} %get-tuple-element.751, f32[3,1024]{1,0:T(4,128)S(1)} %log_add_fusion.2), kind=kLoop, calls=%fused_computation.clone.1 | loop fusion | flops 25165824 | bytes 62939136 | tf_op jit(solution)/shard_map/while/body/eval_jaxpr/convert_element_type | solution.py:175
  531.7 106.1 %all-gather.16.cloned.1.call-done = f32[4096,768]{1,0:T(8,128)} async-done(((f32[1024,768]{1,0:T(8,128)}), f32[4096,768]{1,0:T(8,128)}) %all-gather.16.cloned.1.call-update) | async-done | bytes 12582928 | tf_op jit(solution)/shard_map/while/body/eval_jaxpr/all_gather | solution.py:209
  649.1 21.4 %all_gather.54 = bf16[768,3,192]{2,1,0:T(4,128)(2,1)} all-gather(bf16[96,3,192]{2,1,0:T(4,128)(2,1)S(1)} %get-tuple-element.830), channel_id=1, replica_groups=mesh['shard'=4,'ctx'=2,'tp'=4] {'shard','ctx'}, dimensions={0}, use_global_device_ids=true | all-gather | bytes 995328 | tf_op jit(solution)/shard_map/while/body/eval_jaxpr/all_gather | solution.py:42
  700.2 16.0 %all_gather.53 = bf16[768,192]{1,0:T(8,128)(2,1)} all-gather(bf16[96,192]{1,0:T(8,128)(2,1)} %get-tuple-element.834), channel_id=1, replica_groups=mesh['shard'=4,'ctx'=2,'tp'=4] {'shard','ctx'}, dimensions={0}, use_global_device_ids=true | all-gather | bytes 331776 | tf_op jit(solution)/shard_map/while/body/eval_jaxpr/all_gather | solution.py:43
  758.7 83.5 %all-reduce.9.cloned.1.call-done = f32[1024,768]{1,0:T(8,128)} async-done(((f32[1024,768]{1,0:T(8,128)}), f32[1024,768]{1,0:T(8,128)}) %all-reduce.9.cloned.1.call-update) | async-done | bytes 3145744 | tf_op jit(solution)/shard_map/while/body/eval_jaxpr/psum | solution.py:131
  847.2 11.2 multiply_convert_fusion.4
  863.0 87.2 %all-reduce.11.cloned.1.call-done = f32[1024,768]{1,0:T(8,128)} async-done(((f32[1024,768]{1,0:T(8,128)}), f32[1024,768]{1,0:T(8,128)}) %all-reduce.11.cloned.1.call-update) | async-done | bytes 3145744 | tf_op jit(solution)/shard_map/while/body/eval_jaxpr/psum | solution.py:142
  970.7 86.3 %all-reduce.13.cloned.1.call-done = f32[1024,768]{1,0:T(8,128)} async-done(((f32[1024,768]{1,0:T(8,128)}), f32[1024,768]{1,0:T(8,128)}) %all-reduce.13.cloned.1.call-update) | async-done | bytes 3145744 | tf_op jit(solution)/shard_map/while/body/eval_jaxpr/psum | solution.py:157
  1065.3 11.4 fusion.160
  1076.8 16.4 %multiply_reduce_fusion.14 = (f32[3,1024]{1,0:T(4,128)}, f32[3,1024,2048]{2,1,0:T(8,128)}) fusion(f32[3,1024,2048]{2,1,0:T(8,128)} %get-tuple-element.731, f32[3,1024]{1,0:T(4,128)S(1)} %log_add_fusion.2, bf16[1024,3,64]{0,2,1:T(8,128)(2,1)} %bitcast.227, bf16[2048,3,64]{0,2,1:T(8,128)(2,1)} %bitcast.231), kind=kOutput, calls=%fused_computation.1.clone.1 | convolution fusion | flops 824177664 | bytes 51535872 | tf_op jit(solution)/shard_map/while/body/eval_jaxpr/shd,thd->hst/dot_general | solution.py:171
  1093.1 16.8 %multiply_convert_fusion.5 = bf16[3,1024,2048]{2,1,0:T(8,128)(2,1)S(1)} fusion(f32[3,1024,2048]{2,1,0:T(8,128)} %get-tuple-element.750, f32[3,1024,2048]{2,1,0:T(8,128)} %get-tuple-element.731, f32[3,1024]{1,0:T(4,128)} %get-tuple-element.751, f32[3,1024]{1,0:T(4,128)S(1)} %log_add_fusion.2), kind=kLoop, calls=%fused_computation.clone.1 | loop fusion | flops 25165824 | bytes 62939136 | tf_op jit(solution)/shard_map/while/body/eval_jaxpr/convert_element_type | solution.py:175
  1168.4 104.6 %all-gather.16.cloned.1.call-done = f32[4096,768]{1,0:T(8,128)} async-done(((f32[1024,768]{1,0:T(8,128)}), f32[4096,768]{1,0:T(8,128)}) %all-gather.16.cloned.1.call-update) | async-done | bytes 12582928 | tf_op jit(solution)/shard_map/while/body/eval_jaxpr/all_gather | solution.py:209
  1303.2 42.1 %all-reduce.1 = (f32[3,768]{1,0:T(4,128)S(1)}, f32[3072]{0:T(1024)S(1)}, f32[2,768]{1,0:T(2,128)}, f32[4,768]{1,0:T(4,128)}) all-reduce(f32[3,768]{1,0:T(4,128)S(1)} %dynamic_update_slice.19, f32[3072]{0:T(1024)S(1)} %dynamic_update_slice.20, ...), channel_id=1, replica_groups=mesh['shard'=4,'ctx'=2,'tp'=4] {'shard','ctx','tp'}, use_global_device_ids=true, to_apply=%region_29.30 | all-reduce | flops 9984 | bytes 79872 | tf_op jit(solution)/shard_map/psum | solution.py:258
  1347.9 56.7 %all-reduce.7.cloned.1.call-done = f32[768,2,768]{2,1,0:T(2,128)} async-done(((f32[768,2,768]{2,1,0:T(2,128)}), f32[768,2,768]{2,1,0:T(2,128)}) %all-reduce.7.cloned.1.call-update) | async-done | bytes 4718608
  1406.5 32.5 %reduce-scatter.6.cloned.1.call-done = f32[96,192]{1,0:T(8,128)} async-done(((f32[768,192]{1,0:T(8,128)}), f32[96,192]{1,0:T(8,128)}) %reduce-scatter.6.cloned.1.call-update) | async-done | bytes 73744 | tf_op jit(solution)/shard_map/reduce_scatter | solution.py:247
  1439.0 37.6 %reduce-scatter.4.cloned.1.call-done = f32[96,3,192]{2,0,1:T(8,128)} async-done(((f32[768,3,192]{2,0,1:T(8,128)}), f32[96,3,192]{2,0,1:T(8,128)}) %reduce-scatter.4.cloned.1.call-update) | async-done | bytes 221200 | tf_op jit(solution)/shard_map/reduce_scatter | solution.py:246
  (529 shorter events, 388.5 us)
Async XLA Ops:
  10.9 71.7 %all-gather.12.cloned.1.call-start = ((), (), s32[]{:S(2)}) async-start(), calls=%async_computation.6 | async-start | bytes 2359296 | tf_op jit(solution)/shard_map/while/body/eval_jaxpr/all_gather | solution.py:114
  57.9 149.1 %all-reduce.9.cloned.1.call-start = ((), (), s32[]{:S(2)}) async-start(), calls=%async_computation.7 | async-start | bytes 6291456 | tf_op jit(solution)/shard_map/while/body/eval_jaxpr/psum | solution.py:131
  119.9 92.2 %all-gather.14.cloned.1.call-start = ((), (), s32[]{:S(2)}) async-start(), calls=%async_computation.8 | async-start | bytes 2654208 | tf_op jit(solution)/shard_map/while/body/eval_jaxpr/all_gather | solution.py:48
  120.5 194.5 %all-reduce.11.cloned.1.call-start = ((), (), s32[]{:S(2)}) async-start(), calls=%async_computation.9 | async-start | bytes 6291456 | tf_op jit(solution)/shard_map/while/body/eval_jaxpr/psum | solution.py:142
  120.8 194.2 %copy-start.34 = (f32[768]{0:T(1024)}, f32[768]{0:T(1024)S(1)}, u32[]{:S(2)}) copy-start(f32[768]{0:T(1024)S(1)} %get-tuple-element.733) | copy-start | bytes 9220 | tf_op jit(solution)/shard_map/while
  122.3 192.7 %copy-start.44 = (f32[768]{0:T(1024)}, f32[768]{0:T(1024)S(1)}, u32[]{:S(2)}) copy-start(f32[768]{0:T(1024)S(1)} %get-tuple-element.737) | copy-start | bytes 9220 | tf_op jit(solution)/shard_map/while
  227.6 87.4 %copy-start.47 = (f32[768]{0:T(1024)S(1)}, f32[768]{0:T(1024)}, u32[]{:S(2)}) copy-start(f32[768]{0:T(1024)} %get-tuple-element.736) | copy-start | bytes 9220 | tf_op jit(solution)/shard_map/while
  227.6 194.3 %all-reduce.13.cloned.1.call-start = ((), (), s32[]{:S(2)}) async-start(), calls=%async_computation.10 | async-start | bytes 6291456 | tf_op jit(solution)/shard_map/while/body/eval_jaxpr/psum | solution.py:157
  334.6 159.8 %reduce-scatter.8.cloned.1.call-start = ((), (), s32[]{:S(2)}) async-start(), calls=%async_computation.11 | async-start | bytes 4718592 | tf_op jit(solution)/shard_map/while/body/eval_jaxpr/reduce_scatter | solution.py:187
  481.6 156.3 %all-gather.16.cloned.1.call-start = ((), (), s32[]{:S(2)}) async-start(), calls=%async_computation.12 | async-start | bytes 15728640 | tf_op jit(solution)/shard_map/while/body/eval_jaxpr/all_gather | solution.py:209
  649.0 69.7 %all-gather.12.cloned.1.call-start = ((), (), s32[]{:S(2)}) async-start(), calls=%async_computation.6 | async-start | bytes 2359296 | tf_op jit(solution)/shard_map/while/body/eval_jaxpr/all_gather | solution.py:114
  694.3 147.8 %all-reduce.9.cloned.1.call-start = ((), (), s32[]{:S(2)}) async-start(), calls=%async_computation.7 | async-start | bytes 6291456 | tf_op jit(solution)/shard_map/while/body/eval_jaxpr/psum | solution.py:131
  756.0 91.2 %all-gather.14.cloned.1.call-start = ((), (), s32[]{:S(2)}) async-start(), calls=%async_computation.8 | async-start | bytes 2654208 | tf_op jit(solution)/shard_map/while/body/eval_jaxpr/all_gather | solution.py:48
  756.6 193.5 %all-reduce.11.cloned.1.call-start = ((), (), s32[]{:S(2)}) async-start(), calls=%async_computation.9 | async-start | bytes 6291456 | tf_op jit(solution)/shard_map/while/body/eval_jaxpr/psum | solution.py:142
  757.2 192.9 %copy-start.34 = (f32[768]{0:T(1024)}, f32[768]{0:T(1024)S(1)}, u32[]{:S(2)}) copy-start(f32[768]{0:T(1024)S(1)} %get-tuple-element.733) | copy-start | bytes 9220 | tf_op jit(solution)/shard_map/while
  758.7 191.5 %copy-start.44 = (f32[768]{0:T(1024)}, f32[768]{0:T(1024)S(1)}, u32[]{:S(2)}) copy-start(f32[768]{0:T(1024)S(1)} %get-tuple-element.737) | copy-start | bytes 9220 | tf_op jit(solution)/shard_map/while
  862.7 87.4 %copy-start.47 = (f32[768]{0:T(1024)S(1)}, f32[768]{0:T(1024)}, u32[]{:S(2)}) copy-start(f32[768]{0:T(1024)} %get-tuple-element.736) | copy-start | bytes 9220 | tf_op jit(solution)/shard_map/while
  862.7 194.3 %all-reduce.13.cloned.1.call-start = ((), (), s32[]{:S(2)}) async-start(), calls=%async_computation.10 | async-start | bytes 6291456 | tf_op jit(solution)/shard_map/while/body/eval_jaxpr/psum | solution.py:157
  969.7 159.6 %reduce-scatter.8.cloned.1.call-start = ((), (), s32[]{:S(2)}) async-start(), calls=%async_computation.11 | async-start | bytes 4718592 | tf_op jit(solution)/shard_map/while/body/eval_jaxpr/reduce_scatter | solution.py:187
  1116.7 156.3 %all-gather.16.cloned.1.call-start = ((), (), s32[]{:S(2)}) async-start(), calls=%async_computation.12 | async-start | bytes 15728640 | tf_op jit(solution)/shard_map/while/body/eval_jaxpr/all_gather | solution.py:209
  1289.0 115.6 %all-reduce.7.cloned.1.call-start = ((), (), s32[]{:S(2)}) async-start(), calls=%async_computation.5 | async-start | bytes 9437184
  1297.2 141.8 %reduce-scatter.6.cloned.1.call-start = ((), (), s32[]{:S(2)}) async-start(), calls=%async_computation.4 | async-start | bytes 884736 | tf_op jit(solution)/shard_map/reduce_scatter | solution.py:247
  1299.5 177.1 %reduce-scatter.4.cloned.1.call-start = ((), (), s32[]{:S(2)}) async-start(), calls=%async_computation.3 | async-start | bytes 2654208 | tf_op jit(solution)/shard_map/reduce_scatter | solution.py:246
  1299.6 46.4 %copy-start.67 = (u32[32]{0:T(128)S(1)}, u32[32]{0:T(128)}, u32[]{:S(2)}) copy-start(u32[32]{0:T(128)} %constant.281) | copy-start | bytes 388
  (139 other events, 632.9 us)
Sparse Core Ops, SparseCore 0:
  58.0 9.4 all-gather.11
  120.0 86.9 all-reduce.8
  227.7 87.2 all-reduce.10
  334.7 87.1 all-reduce.12
  481.7 10.8 reduce-scatter.7
  515.2 122.5 all-gather.15
  694.5 8.5 all-gather.11
  756.1 85.9 all-reduce.8
  862.9 87.2 all-reduce.10
  969.8 87.1 all-reduce.12
  1116.8 10.8 reduce-scatter.7
  1150.5 122.4 all-gather.15
Sparse Core Ops, SparseCore 1:
  122.6 31.1 all-gather.13
  758.7 30.1 all-gather.13
  1297.3 107.2 all-reduce.6
  1407.5 31.5 reduce-scatter.5
  1442.0 34.5 reduce-scatter.3
